TPU v7x, 32 devices: a whole 2x2x4 slice. The times are simulated.
32 devices in a mesh: dp: 8 (over y, x, core), tensor: 4 (over z).
Axes of the slice: x: 2, y: 2, z: 4, core: 2. Of those that a mesh axis runs over, the one named last changes fastest.
Arguments:
- inputs: bfloat16 [8, 1024, 2048], P('dp'), may hold values from -6 to 6
- segments: int32 [8, 1024], P('dp'), may hold values from 0 to 3, never falling along the last dimension, each value on 1 to 512 neighbouring positions
- cotangent: bfloat16 [8, 1024, 2048], P('dp'), may hold values from -6 to 6
- w_query: bfloat16 [2048, 2048], P(None, 'tensor'), may hold values from -0.046875 to 0.046875
- w_key: bfloat16 [2048, 2048], P(None, 'tensor'), may hold values from -0.046875 to 0.046875
- w_value: bfloat16 [2048, 2048], P(None, 'tensor'), may hold values from -0.125 to 0.125
- w_out: bfloat16 [2048, 2048], P('tensor'), may hold values from -0.5 to 0.5
- w_gate: bfloat16 [2048, 5120], P(None, 'tensor'), may hold values from -0.125 to 0.125
- w_up: bfloat16 [2048, 5120], P(None, 'tensor'), may hold values from -0.125 to 0.125
- w_down: bfloat16 [5120, 2048], P('tensor'), may hold values from -0.125 to 0.125
- gain_attn: float32 [2048], replicated, may hold values from 0.5 to 1.5
- gain_ffn: float32 [2048], replicated, may hold values from 0.5 to 1.5
- bias_table: float32 [32, 32], P(None, 'tensor'), may hold values from -4 to 4
Outputs:
- output: bfloat16 [8, 1024, 2048], P('dp', 'tensor')
- input_grad: bfloat16 [8, 1024, 2048], P('dp', 'tensor')
- query_grad: float32 [2048, 2048], P(None, 'tensor')
- key_grad: float32 [2048, 2048], P(None, 'tensor')
- value_grad: float32 [2048, 2048], P(None, 'tensor')
- out_grad: float32 [2048, 2048], P('tensor')
- gate_grad: float32 [2048, 5120], P(None, 'tensor')
- up_grad: float32 [2048, 5120], P(None, 'tensor')
- down_grad: float32 [5120, 2048], P('tensor')
- gain_attn_grad: float32 [2048], replicated
- gain_ffn_grad: float32 [2048], replicated
- table_grad: float32 [32, 32], P(None, 'tensor')
Inputs may be any that keep to these rules, and one draw needn't show every extreme that they name: `segments`: each row of 1024 tokens holds 4 documents one after another; document numbers never fall along a row; each document has 1 to 512 tokens and one in every row has exactly 512.
All inputs are finite; a program needn't handle non-finite values.
Results may differ from a plain program's by a relative error of at most 0.024.
Values may be sent and summed in bfloat16 or wider, within the bound.
A program may use at most 320 MiB of HBM per device.

v0:
```python
import jax
import jax.numpy as jnp
from jax import lax
from jax.sharding import PartitionSpec as P

thresholds = (12, 16, 23, 32, 46, 64, 91)
highest = lax.Precision.HIGHEST


def buckets_of(start_row, query_count, length):
    queries = start_row + jnp.arange(query_count, dtype=jnp.int32)
    targets = jnp.arange(length, dtype=jnp.int32)
    offset = targets[None, :] - queries[:, None]
    distance = jnp.abs(offset)
    far_bucket = jnp.full(distance.shape, 8, jnp.int32)
    for bound_value in thresholds:
        far_bucket = far_bucket + (distance >= bound_value).astype(jnp.int32)
    near_bucket = jnp.where(distance < 8, distance, far_bucket)
    return near_bucket + 16 * (offset > 0).astype(jnp.int32)


def bucket_onehot(start_row, query_count, length, bucket_count):
    bucket = buckets_of(start_row, query_count, length).reshape(1, query_count * length)
    labels = jnp.arange(bucket_count, dtype=jnp.int32)[:, None]
    return (bucket == labels).astype(jnp.float32)


def project(left_side, right_side):
    return jnp.dot(left_side, right_side, preferred_element_type=jnp.float32)


def project_back(left_side, right_side):
    return lax.dot_general(
        left_side, right_side, (((1,), (1,)), ((), ())), preferred_element_type=jnp.float32
    )


def weight_term(left_side, right_side):
    return lax.dot_general(
        left_side, right_side, (((0,), (0,)), ((), ())), preferred_element_type=jnp.float32
    )


def norm_scale(signal):
    return lax.rsqrt(jnp.mean(signal * signal, axis=-1, keepdims=True) + 1e-06)


def norm_back(signal, rms_scale, gain_vec, grad_normed):
    grad_hat = grad_normed * gain_vec
    inner_mean = jnp.mean(grad_hat * signal, axis=-1, keepdims=True)
    return rms_scale * (grad_hat - signal * rms_scale * rms_scale * inner_mean)


def gain_term(signal, rms_scale, grad_normed):
    return jnp.sum((grad_normed * signal * rms_scale).reshape(-1, signal.shape[-1]), axis=0)


def score_block(query_block, key_row, bias_block, same_doc):
    raw_scores = jnp.einsum(
        "qhd,khd->hqk", query_block, key_row, preferred_element_type=jnp.float32
    )
    return jnp.where(same_doc[None], raw_scores + bias_block, -1000000000.0)


def shards(
    inputs,
    segments,
    cotangent,
    w_query,
    w_key,
    w_value,
    w_out,
    w_gate,
    w_up,
    w_down,
    gain_attn,
    gain_ffn,
    bias_table,
):
    row_count, length, model_width = inputs.shape
    share_rows = length // lax.axis_size("tensor")
    first_row = lax.axis_index("tensor") * share_rows
    bucket_count, head_count = bias_table.shape
    local_width = w_query.shape[1]
    head_dim = local_width // head_count
    block_rows = min(512, length)
    block_count = length // block_rows
    token_count = row_count * length
    plane = (row_count, length, model_width)

    def take_share(signal):
        return lax.dynamic_slice_in_dim(signal, first_row, share_rows, 1)

    flat_inputs = inputs.reshape(token_count, model_width).astype(jnp.float32)
    scale_attn = norm_scale(flat_inputs)
    normed = (flat_inputs * scale_attn * gain_attn).astype(jnp.bfloat16)
    heads_shape = (row_count, length, head_count, head_dim)
    queries = project(normed, w_query).astype(jnp.bfloat16).reshape(heads_shape)
    key_proj = project(normed, w_key).astype(jnp.bfloat16).reshape(heads_shape)
    value_proj = project(normed, w_value).astype(jnp.bfloat16).reshape(heads_shape)
    table_heads = jnp.transpose(bias_table)
    bias_blocks = []
    for block_index in range(block_count):
        onehot = bucket_onehot(block_index * block_rows, block_rows, length, bucket_count)
        bias_flat = jnp.dot(table_heads, onehot, precision=highest)
        bias_blocks.append(bias_flat.reshape(head_count, block_rows, length))
    row_index = 0
    doc_row = segments[row_index]
    pieces = []
    totals_row = []
    for block_index in range(block_count):
        block_start = block_index * block_rows
        same_doc = doc_row[block_start : block_start + block_rows, None] == doc_row[None, :]
        query_block = queries[row_index, block_start : block_start + block_rows]
        scores = score_block(query_block, key_proj[row_index], bias_blocks[block_index], same_doc)
        row_max = jnp.max(scores, axis=-1, keepdims=True)
        weighted = jnp.exp(scores - row_max)
        row_total = jnp.sum(weighted, axis=-1, keepdims=True)
        softmaxed = (weighted / row_total).astype(jnp.bfloat16)
        totals_row.append(row_max + jnp.log(row_total))
        pieces.append(
            jnp.einsum(
                "hqk,khd->qhd", softmaxed, value_proj[row_index], preferred_element_type=jnp.float32
            ).astype(jnp.bfloat16)
        )
    log_totals = [totals_row]
    mixed_rows = [jnp.concatenate(pieces, axis=0)]
    mixed_heads = jnp.stack(mixed_rows).reshape(token_count, local_width)
    attn_part = project(mixed_heads, w_out)
    attn_total = lax.psum(attn_part.astype(jnp.bfloat16), "tensor").astype(jnp.float32)
    middle = flat_inputs + attn_total
    scale_ffn = norm_scale(middle)
    normed_ffn = (middle * scale_ffn * gain_ffn).astype(jnp.bfloat16)
    gate_pre = project(normed_ffn, w_gate)
    up_pre = project(normed_ffn, w_up)
    hidden = (jax.nn.gelu(gate_pre, approximate=True) * up_pre).astype(jnp.bfloat16)
    ffn_part = project(hidden, w_down)
    ffn_total = lax.psum(ffn_part.astype(jnp.bfloat16), "tensor").astype(jnp.float32)
    output = take_share((middle + ffn_total).reshape(plane)).astype(jnp.bfloat16)
    grad_out = cotangent.reshape(token_count, model_width)
    down_grad = weight_term(hidden, grad_out)
    grad_hidden = project_back(grad_out, w_down)
    normed_again = lax.optimization_barrier(normed_ffn)
    gate_back = project(normed_again, w_gate)
    up_back = project(normed_again, w_up)
    act_value, act_pull = jax.vjp(lambda signal: jax.nn.gelu(signal, approximate=True), gate_back)
    grad_gate = act_pull(grad_hidden * up_back)[0].astype(jnp.bfloat16)
    grad_up = (grad_hidden * act_value).astype(jnp.bfloat16)
    gate_grad = weight_term(normed_ffn, grad_gate)
    up_grad = weight_term(normed_ffn, grad_up)
    norm_ffn_part = project_back(grad_gate, w_gate) + project_back(grad_up, w_up)
    grad_normed_ffn = lax.psum(norm_ffn_part.astype(jnp.bfloat16), "tensor").astype(jnp.float32)
    grad_middle = grad_out.astype(jnp.float32) + norm_back(
        middle, scale_ffn, gain_ffn, grad_normed_ffn
    )
    gain_ffn_part = gain_term(
        take_share(middle.reshape(plane)),
        take_share(scale_ffn.reshape(row_count, length, 1)),
        take_share(grad_normed_ffn.reshape(plane)),
    )
    grad_branch = grad_middle.astype(jnp.bfloat16)
    out_grad = weight_term(mixed_heads, grad_branch)
    grad_mixed = project_back(grad_branch, w_out).astype(jnp.bfloat16).reshape(heads_shape)
    score_sums = [
        jnp.zeros((head_count, block_rows, length), jnp.float32)
        for block_index in range(block_count)
    ]
    row_index = 0
    doc_row = segments[row_index]
    key_row = key_proj[row_index]
    value_row = value_proj[row_index]
    key_sum = jnp.zeros((length, head_count, head_dim), jnp.float32)
    value_sum = jnp.zeros((length, head_count, head_dim), jnp.float32)
    query_pieces = []
    for block_index in range(block_count):
        block_start = block_index * block_rows
        same_doc = doc_row[block_start : block_start + block_rows, None] == doc_row[None, :]
        query_block = queries[row_index, block_start : block_start + block_rows]
        grad_block = grad_mixed[row_index, block_start : block_start + block_rows]
        scores = score_block(query_block, key_row, bias_blocks[block_index], same_doc)
        weights_back = jnp.exp(scores - log_totals[row_index][block_index])
        grad_weights = jnp.einsum(
            "qhd,khd->hqk", grad_block, value_row, preferred_element_type=jnp.float32
        )
        row_delta = jnp.sum(weights_back * grad_weights, axis=-1, keepdims=True)
        grad_scores = weights_back * (grad_weights - row_delta)
        score_sums[block_index] = grad_scores
        scores_low = grad_scores.astype(jnp.bfloat16)
        query_pieces.append(
            jnp.einsum(
                "hqk,khd->qhd", scores_low, key_row, preferred_element_type=jnp.float32
            ).astype(jnp.bfloat16)
        )
        key_sum = key_sum + jnp.einsum(
            "hqk,qhd->khd", scores_low, query_block, preferred_element_type=jnp.float32
        )
        value_sum = value_sum + jnp.einsum(
            "hqk,qhd->khd",
            weights_back.astype(jnp.bfloat16),
            grad_block,
            preferred_element_type=jnp.float32,
        )
    query_rows = [jnp.concatenate(query_pieces, axis=0)]
    key_rows = [key_sum.astype(jnp.bfloat16)]
    value_rows = [value_sum.astype(jnp.bfloat16)]
    grad_query = jnp.stack(query_rows).reshape(token_count, local_width)
    grad_key = jnp.stack(key_rows).reshape(token_count, local_width)
    grad_value = jnp.stack(value_rows).reshape(token_count, local_width)
    table_grad = jnp.zeros((bucket_count, head_count), jnp.float32)
    for block_index in range(block_count):
        onehot = bucket_onehot(block_index * block_rows, block_rows, length, bucket_count)
        table_grad = table_grad + lax.dot_general(
            onehot,
            score_sums[block_index].reshape(head_count, block_rows * length),
            (((1,), (1,)), ((), ())),
            precision=highest,
        )
    query_grad = weight_term(normed, grad_query)
    key_grad = weight_term(normed, grad_key)
    value_grad = weight_term(normed, grad_value)
    norm_attn_part = (
        project_back(grad_query, w_query)
        + project_back(grad_key, w_key)
        + project_back(grad_value, w_value)
    )
    grad_normed_attn = lax.psum(norm_attn_part.astype(jnp.bfloat16), "tensor").astype(jnp.float32)
    grad_input = grad_middle + norm_back(flat_inputs, scale_attn, gain_attn, grad_normed_attn)
    input_grad = take_share(grad_input.reshape(plane)).astype(jnp.bfloat16)
    gain_attn_part = gain_term(
        take_share(flat_inputs.reshape(plane)),
        take_share(scale_attn.reshape(row_count, length, 1)),
        take_share(grad_normed_attn.reshape(plane)),
    )
    gain_attn_grad, gain_ffn_grad = lax.psum((gain_attn_part, gain_ffn_part), ("dp", "tensor"))
    reduced = (
        lax.psum_scatter(
            query_grad.astype(jnp.bfloat16), "dp", scatter_dimension=0, tiled=True
        ).astype(jnp.float32),
        lax.psum_scatter(
            key_grad.astype(jnp.bfloat16), "dp", scatter_dimension=0, tiled=True
        ).astype(jnp.float32),
        lax.psum_scatter(
            value_grad.astype(jnp.bfloat16), "dp", scatter_dimension=0, tiled=True
        ).astype(jnp.float32),
        lax.psum_scatter(
            out_grad.astype(jnp.bfloat16), "dp", scatter_dimension=1, tiled=True
        ).astype(jnp.float32),
        lax.psum_scatter(
            gate_grad.astype(jnp.bfloat16), "dp", scatter_dimension=0, tiled=True
        ).astype(jnp.float32),
        lax.psum_scatter(
            up_grad.astype(jnp.bfloat16), "dp", scatter_dimension=0, tiled=True
        ).astype(jnp.float32),
        lax.psum_scatter(
            down_grad.astype(jnp.bfloat16), "dp", scatter_dimension=1, tiled=True
        ).astype(jnp.float32),
        lax.psum_scatter(
            table_grad.astype(jnp.bfloat16), "dp", scatter_dimension=0, tiled=True
        ).astype(jnp.float32),
    )
    gathered = (
        lax.all_gather(reduced[0].astype(jnp.bfloat16), "dp", axis=0, tiled=True).astype(
            jnp.float32
        ),
        lax.all_gather(reduced[1].astype(jnp.bfloat16), "dp", axis=0, tiled=True).astype(
            jnp.float32
        ),
        lax.all_gather(reduced[2].astype(jnp.bfloat16), "dp", axis=0, tiled=True).astype(
            jnp.float32
        ),
        lax.all_gather(reduced[3].astype(jnp.bfloat16), "dp", axis=1, tiled=True).astype(
            jnp.float32
        ),
        lax.all_gather(reduced[4].astype(jnp.bfloat16), "dp", axis=0, tiled=True).astype(
            jnp.float32
        ),
        lax.all_gather(reduced[5].astype(jnp.bfloat16), "dp", axis=0, tiled=True).astype(
            jnp.float32
        ),
        lax.all_gather(reduced[6].astype(jnp.bfloat16), "dp", axis=1, tiled=True).astype(
            jnp.float32
        ),
        lax.all_gather(reduced[7].astype(jnp.bfloat16), "dp", axis=0, tiled=True).astype(
            jnp.float32
        ),
    )
    return (
        output,
        input_grad,
        gathered[0],
        gathered[1],
        gathered[2],
        gathered[3],
        gathered[4],
        gathered[5],
        gathered[6],
        gain_attn_grad,
        gain_ffn_grad,
        gathered[7],
    )


def solution(mesh):
    return jax.shard_map(
        shards,
        mesh=mesh,
        in_specs=(
            P("dp", None, None),
            P("dp", None),
            P("dp", None, None),
            P(None, "tensor"),
            P(None, "tensor"),
            P(None, "tensor"),
            P("tensor", None),
            P(None, "tensor"),
            P(None, "tensor"),
            P("tensor", None),
            P(),
            P(),
            P(None, "tensor"),
        ),
        out_specs=(
            P("dp", "tensor", None),
            P("dp", "tensor", None),
            P(None, "tensor"),
            P(None, "tensor"),
            P(None, "tensor"),
            P("tensor", None),
            P(None, "tensor"),
            P(None, "tensor"),
            P("tensor", None),
            P(),
            P(),
            P(None, "tensor"),
        ),
        check_vma=False,
    )
```

profile of v0, /device:TPU:0, one launch (start us, length us, event | category | flops | bytes accessed | tf_op | source)
XLA Modules:
  0.0 1494.6 jit_solution(11549578221789818774)
XLA Ops:
  17.8 3.6 convolution_convert_fusion.11
  24.2 23.3 %fusion.1 = f32[524288,8]{0,1:T(8,128)} fusion(f32[32,8]{0,1:T(8,128)S(1)} %copy-done.45, s32[524288]{0:T(1024)S(1)} %fusion.51), kind=kOutput, calls=%fused_computation.2 | convolution fusion | flops 1627389952 | bytes 18875392 | tf_op jit(solution)/shard_map/dot_general | solution.py:105
  49.1 23.8 %fusion.3 = f32[524288,8]{0,1:T(8,128)} fusion(f32[32,8]{0,1:T(8,128)S(1)} %copy-done.45, s32[524288]{0:T(1024)S(1)} %fusion.50), kind=kOutput, calls=%fused_computation.5 | convolution fusion | flops 1627389952 | bytes 18875392 | tf_op jit(solution)/shard_map/dot_general | solution.py:105
  73.6 21.5 %fusion.84 = (f32[8,512]{1,0:T(8,128)S(1)}, f32[8,512,1024]{2,1,0:T(8,128)}) fusion(f32[1,8,512,1024]{3,1,2,0:T(8,128)} %bitcast.182, bf16[1024,8,64]{0,2,1:T(8,128)(2,1)S(1)} %bitcast.183, bf16[1,1024,8,64]{1,3,2,0:T(8,128)(2,1)S(1)} %bitcast.193, pred[512,1024]{1,0:T(8,128)(4,1)S(1)} %get-tuple-element.52), kind=kOutput, calls=%fused_computation.152 | convolution fusion | flops 549449728 | bytes 35667968 | tf_op jit(solution)/shard_map/qhd,khd->hqk/dot_general | solution.py:59
  95.1 7.8 fusion.11
  105.7 3.8 fusion.72
  109.6 21.5 %fusion.85 = (f32[8,512]{1,0:T(8,128)S(1)}, f32[8,512,1024]{2,1,0:T(8,128)}) fusion(f32[1,8,512,1024]{3,1,2,0:T(8,128)} %bitcast.181, bf16[1024,8,64]{0,2,1:T(8,128)(2,1)S(1)} %bitcast.184, bf16[1,1024,8,64]{1,3,2,0:T(8,128)(2,1)S(1)} %bitcast.194, pred[512,1024]{1,0:T(8,128)(4,1)S(1)} %get-tuple-element.51), kind=kOutput, calls=%fused_computation.153 | convolution fusion | flops 549449728 | bytes 35667968 | tf_op jit(solution)/shard_map/qhd,khd->hqk/dot_general | solution.py:59
  131.1 7.8 fusion.10
  141.7 3.8 fusion.71
  146.6 4.4 convolution_convert_fusion.4
  151.5 157.4 %all-reduce.7.cloned.1.call-done = bf16[1024,2048]{1,0:T(8,128)(2,1)} async-done(((bf16[1024,2048]{1,0:T(8,128)(2,1)}), bf16[1024,2048]{1,0:T(8,128)(2,1)}) %all-reduce.7.cloned.1.call-update) | async-done | bytes 4194320 | tf_op jit(solution)/shard_map/psum | solution.py:130
  308.9 5.0 multiply_reduce_fusion.3
  317.7 7.3 fusion.87
  324.9 11.4 multiply_convert_fusion.2
  336.4 13.3 fusion.32
  349.6 7.8 fusion.88
  357.5 11.2 add_convert_fusion.1
  368.8 154.1 %all-reduce.9.cloned.1.call-done = bf16[1024,2048]{1,0:T(8,128)(2,1)} async-done(((bf16[1024,2048]{1,0:T(8,128)(2,1)}), bf16[1024,2048]{1,0:T(8,128)(2,1)}) %all-reduce.9.cloned.1.call-update) | async-done | bytes 4194320 | tf_op jit(solution)/shard_map/psum | solution.py:152
  522.8 6.7 multiply_reduce_fusion.2
  531.1 10.1 multiply_add_fusion
  541.2 6.9 fusion.64
  548.1 13.4 multiply_reduce_fusion.1
  561.5 4.2 fusion.14
  565.7 8.8 add_convert_fusion.2
  575.5 4.4 convolution_convert_fusion.6
  580.0 18.7 %fusion.42 = (f32[1,8,512,1024]{3,2,1,0:T(8,128)}, bf16[8,512,1024]{2,1,0:T(8,128)(2,1)S(1)}) fusion(f32[8,512,1024]{2,1,0:T(8,128)} %get-tuple-element.68, f32[8,512]{1,0:T(8,128)S(1)} %get-tuple-element.67, f32[8,512,1024]{2,1,0:T(8,128)} %get-tuple-element.62, f32[8,512]{1,0:T(8,128)S(1)} %log_add_fusion.1), kind=kLoop, calls=%fused_computation.75 | loop fusion | flops 16777216 | bytes 58753024
  602.0 7.1 convolution_convert_fusion.5
  609.1 11.9 multiply_reduce_fusion
  621.0 19.4 %fusion.44 = (f32[1,8,512,1024]{3,2,1,0:T(8,128)}, bf16[8,512,1024]{2,1,0:T(8,128)(2,1)S(1)}) fusion(f32[8,512,1024]{2,1,0:T(8,128)} %get-tuple-element.66, f32[8,512]{1,0:T(8,128)S(1)} %get-tuple-element.65, f32[8,512,1024]{2,1,0:T(8,128)} %get-tuple-element.60, f32[8,512]{1,0:T(8,128)S(1)} %log_add_fusion), kind=kLoop, calls=%fused_computation.77 | loop fusion | flops 16777216 | bytes 58753024
  645.7 4.2 convolution_convert_fusion.7
  650.1 6.3 fusion.69
  659.2 4.2 convolution_convert_fusion.8
  663.5 10.0 convolution_convert_fusion.2
  673.5 9.9 convolution_convert_fusion.1
  683.5 9.0 fusion.86
  692.6 9.1 fusion.41
  703.2 7.5 convolution_convert_fusion
  712.7 42.1 %reduce-scatter.8.cloned.1.call-done = bf16[256,512]{1,0:T(8,128)(2,1)} async-done(((bf16[2048,512]{1,0:T(8,128)(2,1)}), bf16[256,512]{1,0:T(8,128)(2,1)}) %reduce-scatter.8.cloned.1.call-update) | async-done | bytes 262160 | tf_op jit(solution)/shard_map/reduce_scatter | solution.py:236
  754.9 10.4 convolution_convert_fusion.3
  770.1 6.3 add_convert_fusion
  776.5 38.9 %reduce-scatter.16.cloned.1.call-done = bf16[256,1280]{1,0:T(8,128)(2,1)} async-done(((bf16[2048,1280]{1,0:T(8,128)(2,1)}), bf16[256,1280]{1,0:T(8,128)(2,1)}) %reduce-scatter.16.cloned.1.call-update) | async-done | bytes 655376 | tf_op jit(solution)/shard_map/reduce_scatter | solution.py:248
  815.4 60.3 %reduce-scatter.18.cloned.1.call-done = bf16[256,1280]{1,0:T(8,128)(2,1)} async-done(((bf16[2048,1280]{1,0:T(8,128)(2,1)}), bf16[256,1280]{1,0:T(8,128)(2,1)}) %reduce-scatter.18.cloned.1.call-update) | async-done | bytes 655376 | tf_op jit(solution)/shard_map/reduce_scatter | solution.py:251
  875.8 59.9 %reduce-scatter.20.cloned.1.call-done = bf16[1280,256]{1,0:T(8,128)(2,1)} async-done(((bf16[1280,2048]{1,0:T(8,128)(2,1)}), bf16[1280,256]{1,0:T(8,128)(2,1)}) %reduce-scatter.20.cloned.1.call-update) | async-done | bytes 655376 | tf_op jit(solution)/shard_map/reduce_scatter | solution.py:254
  935.8 6.7 convert_element_type.351
  944.5 18.4 %copy.33 = f32[1,8,512,1024]{3,1,2,0:T(8,128)} copy(f32[1,8,512,1024]{3,2,1,0:T(8,128)} %get-tuple-element.40) | data formatting | bytes 33554432
  962.9 18.1 %copy.34 = f32[1,8,512,1024]{3,1,2,0:T(8,128)} copy(f32[1,8,512,1024]{3,2,1,0:T(8,128)} %get-tuple-element.42) | data formatting | bytes 33554432
  981.0 34.5 %fusion = f32[32,8]{1,0:T(8,128)S(1)} fusion(f32[8,524288]{1,0:T(8,128)} %bitcast.188, s32[524288]{0:T(1024)S(1)} %copy-done.21), kind=kOutput, calls=%fused_computation.1 | convolution fusion | flops 1627389952 | bytes 18875392 | tf_op jit(solution)/shard_map/dot_general | solution.py:212
  1015.5 34.6 %fusion.74 = bf16[32,8]{1,0:T(8,128)(2,1)S(1)} fusion(f32[32,8]{1,0:T(8,128)S(1)} %fusion, f32[8,524288]{1,0:T(8,128)} %bitcast.187, s32[524288]{0:T(1024)S(1)} %copy-done.23), kind=kOutput, calls=%fused_computation.129 | convolution fusion | flops 1627390464 | bytes 18875904 | tf_op jit(solution)/shard_map/dot_general | solution.py:212
  1050.2 12.6 all-reduce
  1062.9 9.7 all-gather
  1073.2 6.6 convert_element_type.389
  1079.8 4.2 convert_element_type.415
  1084.0 4.1 convert_element_type.417
  1088.2 4.2 convert_element_type.413
  1092.4 4.2 convert_element_type.411
  1096.6 253.2 %all-reduce.11.cloned.1.call-done = (bf16[1024,2048]{1,0:T(8,128)(2,1)}, bf16[1024,2048]{1,0:T(8,128)(2,1)}) async-done(((bf16[1024,2048]{1,0:T(8,128)(2,1)}, bf16[1024,2048]{1,0:T(8,128)(2,1)}), (bf16[1024,2048]{1,0:T(8,128)(2,1)}, bf16[1024,2048]{1,0:T(8,128)(2,1)})) %all-reduce.11.cloned.1.call-update) | async-done | bytes 8388624 | tf_op jit(solution)/shard_map/psum | solution.py:138
  1354.6 7.1 fusion.21
  1361.7 6.8 fusion.56
  1368.6 39.7 %all-reduce.1 = (f32[2048]{0:T(1024)}, f32[2048]{0:T(1024)}) all-reduce(f32[2048]{0:T(1024)S(1)} %get-tuple-element.57, f32[2048]{0:T(1024)S(1)} %get-tuple-element.70), channel_id=1, replica_groups=mesh['dp'=8,'tensor'=4] {'dp','tensor'}, use_global_device_ids=true, to_apply=%region_22.23 | all-reduce | flops 4096 | bytes 32768 | tf_op jit(solution)/shard_map/psum | solution.py:234
  1408.2 7.4 convert_element_type.419
  1415.6 20.0 %all-gather.19.cloned.1.call-done = bf16[2048,1280]{1,0:T(8,128)(2,1)} async-done(((bf16[256,1280]{1,0:T(8,128)(2,1)}), bf16[2048,1280]{1,0:T(8,128)(2,1)}) %all-gather.19.cloned.1.call-update) | async-done | bytes 5242896 | tf_op jit(solution)/shard_map/all_gather | solution.py:277
  1435.6 7.5 convert_element_type.421
  1443.2 36.4 %all-gather.21.cloned.1.call-done = bf16[1280,2048]{1,0:T(8,128)(2,1)} async-done(((bf16[1280,256]{1,0:T(8,128)(2,1)}), bf16[1280,2048]{1,0:T(8,128)(2,1)}) %all-gather.21.cloned.1.call-update) | async-done | bytes 5242896 | tf_op jit(solution)/shard_map/all_gather | solution.py:280
  1479.6 8.0 convert_element_type.423
  (204 shorter events, 56.2 us)
Async XLA Ops:
  7.2 139.4 %copy-start = (bf16[512,2048]{1,0:T(8,128)(2,1)S(1)}, bf16[512,2048]{1,0:T(8,128)(2,1)}, u32[]{:S(2)}) copy-start(bf16[512,2048]{1,0:T(8,128)(2,1)} %param.19) | copy-start | bytes 6291460
  7.2 301.7 %all-reduce.7.cloned.1.call-start = ((), (), s32[]{:S(2)}) async-start(), calls=%async_computation.7 | async-start | bytes 8388608 | tf_op jit(solution)/shard_map/psum | solution.py:130
  7.3 3.2 copy-start.46
  10.5 6.7 copy-start.42
  13.1 96.5 %copy-start.24 = (bf16[1024,512]{0,1:T(8,128)(2,1)}, bf16[1024,512]{0,1:T(8,128)(2,1)S(1)}, u32[]{:S(2)}) copy-start(bf16[1024,512]{0,1:T(8,128)(2,1)S(1)} %convolution_convert_fusion.10) | copy-start | bytes 3145732
  15.7 93.9 %copy-start.17 = (bf16[1024,512]{0,1:T(8,128)(2,1)}, bf16[1024,512]{0,1:T(8,128)(2,1)S(1)}, u32[]{:S(2)}) copy-start(bf16[1024,512]{0,1:T(8,128)(2,1)S(1)} %convolution_convert_fusion.9) | copy-start | bytes 3145732
  24.2 23.3 %copy-start.20 = (s32[524288]{0:T(1024)}, s32[524288]{0:T(1024)S(1)}, u32[]{:S(2)}) copy-start(s32[524288]{0:T(1024)S(1)} %fusion.51) | copy-start | bytes 6291460
  49.1 23.8 %copy-start.22 = (s32[524288]{0:T(1024)}, s32[524288]{0:T(1024)S(1)}, u32[]{:S(2)}) copy-start(s32[524288]{0:T(1024)S(1)} %fusion.50) | copy-start | bytes 6291460
  73.6 29.4 %copy-start.30 = (bf16[1024,512]{0,1:T(8,128)(2,1)S(1)}, bf16[1024,512]{0,1:T(8,128)(2,1)}, u32[]{:S(2)}) copy-start(bf16[1024,512]{0,1:T(8,128)(2,1)} %convolution_convert_fusion.11) | copy-start | bytes 3145732
  95.1 10.6 copy-start.2
  131.0 10.6 copy-start.3
  151.0 162.9 %copy-start.40 = (f32[2048]{0:T(1024)S(1)}, f32[2048]{0:T(1024)}, u32[]{:S(2)}) copy-start(f32[2048]{0:T(1024)} %param.24) | copy-start | bytes 24580
  151.1 371.8 %all-reduce.9.cloned.1.call-start = ((), (), s32[]{:S(2)}) async-start(), calls=%async_computation.8 | async-start | bytes 8388608 | tf_op jit(solution)/shard_map/psum | solution.py:152
  308.9 5.1 copy-start.5
  308.9 5.9 copy-start.14
  308.9 8.7 slice-start.4
  314.8 214.8 %copy-start.41 = (f32[1024]{0:T(1024)}, f32[1024]{0:T(1024)S(1)}, u32[]{:S(2)}) copy-start(f32[1024]{0:T(1024)S(1)} %add_rsqrt_fusion) | copy-start | bytes 12292
  317.6 18.7 %copy-start.26 = (bf16[1024,2048]{1,0:T(8,128)(2,1)}, bf16[1024,2048]{1,0:T(8,128)(2,1)S(1)}, u32[]{:S(2)}) copy-start(bf16[1024,2048]{1,0:T(8,128)(2,1)S(1)} %multiply_convert_fusion) | copy-start | bytes 12582916
  317.6 7.3 copy-start.31
  336.4 21.1 %copy-start.54 = (bf16[1024,1280]{1,0:T(8,128)(2,1)}, bf16[1024,1280]{1,0:T(8,128)(2,1)S(1)}, u32[]{:S(2)}) copy-start(bf16[1024,1280]{1,0:T(8,128)(2,1)S(1)} %get-tuple-element.63) | copy-start | bytes 7864324
  349.6 7.9 copy-start.55
  368.7 342.1 %reduce-scatter.12.cloned.1.call-start = ((), (), s32[]{:S(2)}) async-start(), calls=%async_computation.13 | async-start | bytes 2359296 | tf_op jit(solution)/shard_map/reduce_scatter | solution.py:242
  522.8 6.8 copy-start.6
  522.8 7.1 copy-start.15
  522.8 8.3 copy-start.16
  541.2 20.2 %slice-start = ((s8[16777216]{0:T(1024)(128)(4,1)}), s8[4194304]{0:T(1024)(128)(4,1)S(1)}, s32[]{:S(2)}) async-start(s8[16777216]{0:T(1024)(128)(4,1)} %bitcast.179), calls=%async_computation.24 | async-start | bytes 8388608
  541.2 20.2 %slice-start.1 = ((s8[16777216]{0:T(1024)(128)(4,1)}), s8[4194304]{0:T(1024)(128)(4,1)S(1)}, s32[]{:S(2)}) async-start(s8[16777216]{0:T(1024)(128)(4,1)} %bitcast.179), calls=%async_computation.25 | async-start | bytes 8388608
  548.1 13.4 slice-start.2
  548.1 13.4 slice-start.3
  565.7 9.9 copy-start.7
  565.7 9.9 copy-start.43
  565.7 9.8 copy-start.47
  579.9 131.4 %reduce-scatter.14.cloned.1.call-start = ((), (), s32[]{:S(2)}) async-start(), calls=%async_computation.15 | async-start | bytes 2359296 | tf_op jit(solution)/shard_map/reduce_scatter | solution.py:245
  580.0 18.7 %copy-start.25 = (bf16[1024,512]{0,1:T(8,128)(2,1)S(1)}, bf16[1024,512]{0,1:T(8,128)(2,1)}, u32[]{:S(2)}) copy-start(bf16[1024,512]{0,1:T(8,128)(2,1)} %copy-done.24) | copy-start | bytes 3145732
  598.6 3.3 copy-start.13
  598.7 3.3 copy-start.39
  621.0 91.1 %reduce-scatter.10.cloned.1.call-start = ((), (), s32[]{:S(2)}) async-start(), calls=%async_computation.11 | async-start | bytes 2359296 | tf_op jit(solution)/shard_map/reduce_scatter | solution.py:239
  640.4 4.3 copy-start.11
  640.4 5.3 copy-start.8
  645.7 4.3 copy-start.18
  650.0 104.8 %reduce-scatter.8.cloned.1.call-start = ((), (), s32[]{:S(2)}) async-start(), calls=%async_computation.9 | async-start | bytes 2359296 | tf_op jit(solution)/shard_map/reduce_scatter | solution.py:236
  650.1 6.3 copy-start.12
  659.2 4.2 copy-start.36
  663.4 151.9 %reduce-scatter.16.cloned.1.call-start = ((), (), s32[]{:S(2)}) async-start(), calls=%async_computation.17 | async-start | bytes 5898240 | tf_op jit(solution)/shard_map/reduce_scatter | solution.py:248
  673.5 202.2 %reduce-scatter.18.cloned.1.call-start = ((), (), s32[]{:S(2)}) async-start(), calls=%async_computation.19 | async-start | bytes 5898240 | tf_op jit(solution)/shard_map/reduce_scatter | solution.py:251
  683.5 252.3 %reduce-scatter.20.cloned.1.call-start = ((), (), s32[]{:S(2)}) async-start(), calls=%async_computation.21 | async-start | bytes 5898240 | tf_op jit(solution)/shard_map/reduce_scatter | solution.py:254
  683.5 9.1 copy-start.27
  692.6 10.6 copy-start.32
  710.7 369.1 %all-gather.13.cloned.1.call-start = ((), (), s32[]{:S(2)}) async-start(), calls=%async_computation.14 | async-start | bytes 2359296 | tf_op jit(solution)/shard_map/all_gather | solution.py:268
  711.3 372.7 %all-gather.15.cloned.1.call-start = ((), (), s32[]{:S(2)}) async-start(), calls=%async_computation.16 | async-start | bytes 2359296 | tf_op jit(solution)/shard_map/all_gather | solution.py:271
  712.0 376.1 %all-gather.11.cloned.1.call-start = ((), (), s32[]{:S(2)}) async-start(), calls=%async_computation.12 | async-start | bytes 2359296 | tf_op jit(solution)/shard_map/all_gather | solution.py:265
  712.6 379.7 %all-gather.9.cloned.1.call-start = ((), (), s32[]{:S(2)}) async-start(), calls=%async_computation.10 | async-start | bytes 2359296 | tf_op jit(solution)/shard_map/all_gather | solution.py:262
  754.8 10.5 copy-start.34
  754.8 595.0 %all-reduce.11.cloned.1.call-start = ((), (), s32[]{:S(2)}) async-start(), calls=%async_computation.23 | async-start | bytes 16777216 | tf_op jit(solution)/shard_map/psum | solution.py:138
  754.9 10.4 copy-start.49
  776.4 631.8 %all-gather.17.cloned.1.call-start = ((), (), s32[]{:S(2)}) async-start(), calls=%async_computation.18 | async-start | bytes 5898240 | tf_op jit(solution)/shard_map/all_gather | solution.py:274
  815.4 620.2 %all-gather.19.cloned.1.call-start = ((), (), s32[]{:S(2)}) async-start(), calls=%async_computation.20 | async-start | bytes 5898240 | tf_op jit(solution)/shard_map/all_gather | solution.py:277
  875.7 603.9 %all-gather.21.cloned.1.call-start = ((), (), s32[]{:S(2)}) async-start(), calls=%async_computation.22 | async-start | bytes 5898240 | tf_op jit(solution)/shard_map/all_gather | solution.py:280
  935.8 6.8 copy-start.52
  962.9 18.1 %copy-start.21 = (s32[524288]{0:T(1024)S(1)}, s32[524288]{0:T(1024)}, u32[]{:S(2)}) copy-start(s32[524288]{0:T(1024)} %copy-done.20) | copy-start | bytes 6291460
  981.0 34.5 %copy-start.23 = (s32[524288]{0:T(1024)S(1)}, s32[524288]{0:T(1024)}, u32[]{:S(2)}) copy-start(s32[524288]{0:T(1024)} %copy-done.22) | copy-start | bytes 6291460
  1349.8 3.4 copy-start.10
  1349.8 4.7 copy-start.19
  1435.6 52.0 %copy-start.1 = (bf16[512,2048]{1,0:T(8,128)(2,1)S(1)}, bf16[512,2048]{1,0:T(8,128)(2,1)}, u32[]{:S(2)}) copy-start(bf16[512,2048]{1,0:T(8,128)(2,1)} %param.19) | copy-start | bytes 6291460
  (15 other events, 30.4 us)
Sparse Core Ops, SparseCore 0:
  151.2 157.6 all-reduce.6
  368.8 153.9 all-reduce.8
  580.1 40.2 reduce-scatter.11
  623.8 41.2 reduce-scatter.13
  668.2 41.2 reduce-scatter.9
  713.5 41.2 reduce-scatter.7
  758.7 56.5 reduce-scatter.15
  819.1 56.5 reduce-scatter.17
  879.1 56.5 reduce-scatter.19
  937.6 27.8 all-gather.12
  967.6 28.1 all-gather.14
  997.7 27.8 all-gather.10
  1027.7 27.9 all-gather.8
  1058.3 291.5 all-reduce.10
  1351.7 40.4 all-gather.16
  1394.1 41.4 all-gather.18
  1437.5 42.0 all-gather.20
where the time goes:
time: 1500 us; the launch traced here: 1490 us
  waiting for transfers between devices  824 us (55%)
  matrix products  375 us (25%)
  other arithmetic  155 us (10%)
  blocking collectives  62 us (4%)
  local copies, waits for them, and re-layouts  61.4 us (4%)
  between operations  15.9 us (1%)
    psum x1, waiting for transfers between devices, shards(): lax.psum(ffn_part.astype(jnp.bfloat16), 'tensor').astype(jnp.float32)  253 us
    psum x1, waiting for transfers between devices, shards(): lax.psum(attn_part.astype(jnp.bfloat16), 'tensor').astype(jnp.float32)  157 us
    psum x1, waiting for transfers between devices, shards(): lax.psum(norm_ffn_part.astype(jnp.bfloat16), 'tensor').astype(jnp.float32)  154 us
    dot_general x2, matrix products, shards(): lax.dot_general(onehot, score_sums[block_index].reshape(head_count, block...  69.2 us
    dot_general x9, matrix products, project(): return jnp.dot(left_side, right_side, preferred_element_type=jnp.float32)  62.2 us
    unnamed x133, local copies, waits for them, and re-layouts  60.4 us
    reduce_scatter x1, waiting for transfers between devices, shards(): lax.psum_scatter(up_grad.astype(jnp.bfloat16), 'dp', scatter_dimension=0,...  60.3 us
    reduce_scatter x1, waiting for transfers between devices, shards(): lax.psum_scatter(down_grad.astype(jnp.bfloat16), 'dp', scatter_dimension=...  59.9 us
  transfers between devices with their start and end apart: 17, of which 9 were waited for; matrix products, arithmetic and copies ran while one was open for 21% of the time, Pallas kernels for 0%

commit v1 on v0

--- a/solution.py
+++ b/solution.py
@@ -149,7 +149,9 @@
     gate_grad = weight_term(normed_ffn, grad_gate)
     up_grad = weight_term(normed_ffn, grad_up)
     norm_ffn_part = project_back(grad_gate, w_gate) + project_back(grad_up, w_up)
-    grad_normed_ffn = lax.psum(norm_ffn_part.astype(jnp.bfloat16), "tensor").astype(jnp.float32)
+    grad_normed_ffn = jnp.sum(
+        jax.lax.all_gather(norm_ffn_part.astype(jnp.bfloat16), "tensor"), axis=0
+    ).astype(jnp.float32)
     grad_middle = grad_out.astype(jnp.float32) + norm_back(
         middle, scale_ffn, gain_ffn, grad_normed_ffn
     )

time: 1500 us -> 1630 us (1.087)
  waiting for transfers between devices: 824 us -> 937 us
    all_gather x0 -> x1, waiting for transfers between devices: none -> 237 us  [shards(): jax.lax.all_gather(norm_ffn_part.astype(jnp.bfloat16), 'tensor')]
    psum x1 -> x0, waiting for transfers between devices: 154 us -> none  [shards(): lax.psum(norm_ffn_part.astype(jnp.bfloat16), 'tensor').astype(jnp.float32)]
    reduce_scatter x1, waiting for transfers between devices: 60.3 us -> 0.02 us  [shards(): lax.psum_scatter(up_grad.astype(jnp.bfloat16), 'dp', scatter_dimension=0,...]
    reduce_scatter x1, waiting for transfers between devices: 0.02 us -> 45 us  [shards(): lax.psum_scatter(key_grad.astype(jnp.bfloat16), 'dp', scatter_dimension=0...]
    reduce_scatter x1, waiting for transfers between devices: 0.02 us -> 44.8 us  [shards(): lax.psum_scatter(out_grad.astype(jnp.bfloat16), 'dp', scatter_dimension=1...]
    reduce_scatter x1, waiting for transfers between devices: 0.02 us -> 44.1 us  [shards(): lax.psum_scatter(value_grad.astype(jnp.bfloat16), 'dp', scatter_dimension...]
    reduce_scatter x1, waiting for transfers between devices: 38.9 us -> 0.02 us  [shards(): lax.psum_scatter(gate_grad.astype(jnp.bfloat16), 'dp', scatter_dimension=...]
    reduce_scatter x1, waiting for transfers between devices: 59.9 us -> 24.5 us  [shards(): lax.psum_scatter(down_grad.astype(jnp.bfloat16), 'dp', scatter_dimension=...]
  transfers between devices with their start and end apart: 17 -> 17, of which waited for: 9 -> 11; matrix products, arithmetic and copies ran while one was open for 21% -> 23% of each run, Pallas kernels for 0% -> 0%
where the time goes in v1:
time: 1630 us; the launch traced here: 1620 us
  waiting for transfers between devices  937 us (57%)
  matrix products  370 us (23%)
  other arithmetic  171 us (10%)
  local copies, waits for them, and re-layouts  63.8 us (4%)
  blocking collectives  62 us (4%)
    psum x1, waiting for transfers between devices, shards(): lax.psum(ffn_part.astype(jnp.bfloat16), 'tensor').astype(jnp.float32)  251 us
    all_gather x1, waiting for transfers between devices, shards(): jax.lax.all_gather(norm_ffn_part.astype(jnp.bfloat16), 'tensor')  237 us
    psum x1, waiting for transfers between devices, shards(): lax.psum(attn_part.astype(jnp.bfloat16), 'tensor').astype(jnp.float32)  157 us
    dot_general x2, matrix products, shards(): lax.dot_general(onehot, score_sums[block_index].reshape(head_count, block...  69.1 us
    unnamed x145, local copies, waits for them, and re-layouts  63.5 us
    dot_general x9, matrix products, project(): return jnp.dot(left_side, right_side, preferred_element_type=jnp.float32)  62.1 us
    dot_general x7, matrix products, weight_term(): lax.dot_general(left_side, right_side, (((0,), (0,)), ((), ())), preferre...  47.4 us
    dot_general x7, matrix products, project_back(): lax.dot_general(left_side, right_side, (((1,), (1,)), ((), ())), preferre...  47.4 us
  transfers between devices with their start and end apart: 17, of which 11 were waited for; matrix products, arithmetic and copies ran while one was open for 23% of the time, Pallas kernels for 0%

profile of v1, /device:TPU:0, one launch (start us, length us, event | category | flops | bytes accessed | tf_op | source)
XLA Modules:
  0.0 1621.1 jit_solution(16702438830401462655)
XLA Ops:
  24.2 23.2 %fusion.1 = f32[524288,8]{0,1:T(8,128)} fusion(f32[32,8]{0,1:T(8,128)S(1)} %copy-done.47, s32[524288]{0:T(1024)S(1)} %fusion.51), kind=kOutput, calls=%fused_computation.2 | convolution fusion | flops 1627389952 | bytes 18875392 | tf_op jit(solution)/shard_map/dot_general | solution.py:105
  49.1 23.7 %fusion.3 = f32[524288,8]{0,1:T(8,128)} fusion(f32[32,8]{0,1:T(8,128)S(1)} %copy-done.47, s32[524288]{0:T(1024)S(1)} %fusion.50), kind=kOutput, calls=%fused_computation.5 | convolution fusion | flops 1627389952 | bytes 18875392 | tf_op jit(solution)/shard_map/dot_general | solution.py:105
  73.4 21.5 %fusion.84 = (f32[8,512]{1,0:T(8,128)S(1)}, f32[8,512,1024]{2,1,0:T(8,128)}) fusion(f32[1,8,512,1024]{3,1,2,0:T(8,128)} %bitcast.183, bf16[1024,8,64]{0,2,1:T(8,128)(2,1)S(1)} %bitcast.186, bf16[1,1024,8,64]{1,3,2,0:T(8,128)(2,1)S(1)} %bitcast.197, pred[512,1024]{1,0:T(8,128)(4,1)S(1)} %get-tuple-element.52), kind=kOutput, calls=%fused_computation.152 | convolution fusion | flops 549449728 | bytes 35667968 | tf_op jit(solution)/shard_map/qhd,khd->hqk/dot_general | solution.py:59
  94.9 7.8 fusion.11
  109.4 21.6 %fusion.85 = (f32[8,512]{1,0:T(8,128)S(1)}, f32[8,512,1024]{2,1,0:T(8,128)}) fusion(f32[1,8,512,1024]{3,1,2,0:T(8,128)} %bitcast.182, bf16[1024,8,64]{0,2,1:T(8,128)(2,1)S(1)} %bitcast.187, bf16[1,1024,8,64]{1,3,2,0:T(8,128)(2,1)S(1)} %bitcast.198, pred[512,1024]{1,0:T(8,128)(4,1)S(1)} %get-tuple-element.51), kind=kOutput, calls=%fused_computation.153 | convolution fusion | flops 549449728 | bytes 35667968 | tf_op jit(solution)/shard_map/qhd,khd->hqk/dot_general | solution.py:59
  131.0 7.8 fusion.10
  141.6 3.8 fusion.71
  146.5 4.4 convolution_convert_fusion.4
  151.4 157.4 %all-reduce.6.cloned.1.call-done = bf16[1024,2048]{1,0:T(8,128)(2,1)} async-done(((bf16[1024,2048]{1,0:T(8,128)(2,1)}), bf16[1024,2048]{1,0:T(8,128)(2,1)}) %all-reduce.6.cloned.1.call-update) | async-done | bytes 4194320 | tf_op jit(solution)/shard_map/psum | solution.py:130
  308.8 5.0 multiply_reduce_fusion.3
  317.5 7.3 fusion.87
  324.8 11.4 multiply_convert_fusion.2
  336.3 13.3 fusion.32
  349.5 7.8 fusion.88
  357.4 11.2 add_convert_fusion.1
  368.6 9.8 convolution_convert_fusion.2
  378.5 10.6 convolution_convert_fusion.1
  389.2 9.2 fusion.86
  398.4 9.1 fusion.41
  409.0 7.4 convolution_convert_fusion
  417.2 237.3 %all-gather.25.cloned.1.call-done = bf16[4096,2048]{1,0:T(8,128)(2,1)} async-done(((bf16[1024,2048]{1,0:T(8,128)(2,1)}), bf16[4096,2048]{1,0:T(8,128)(2,1)}) %all-gather.25.cloned.1.call-update) | async-done | bytes 16777232 | tf_op jit(solution)/shard_map/all_gather | solution.py:153
  654.5 12.5 reduce_sum.106
  667.0 7.8 multiply_reduce_fusion.2
  674.9 13.6 multiply_add_fusion
  688.5 6.0 fusion.64
  698.0 8.3 add_convert_fusion.2
  707.4 4.2 convolution_convert_fusion.6
  711.6 11.3 multiply_reduce_fusion.1
  723.0 19.4 %fusion.42 = (f32[1,8,512,1024]{3,2,1,0:T(8,128)}, bf16[8,512,1024]{2,1,0:T(8,128)(2,1)S(1)}) fusion(f32[8,512,1024]{2,1,0:T(8,128)} %get-tuple-element.68, f32[8,512]{1,0:T(8,128)S(1)} %get-tuple-element.67, f32[8,512,1024]{2,1,0:T(8,128)} %get-tuple-element.62, f32[8,512]{1,0:T(8,128)S(1)} %log_add_fusion.1), kind=kLoop, calls=%fused_computation.75 | loop fusion | flops 16777216 | bytes 58753024
  747.3 7.1 convolution_convert_fusion.5
  754.5 11.9 multiply_reduce_fusion
  766.4 18.0 %fusion.44 = (f32[1,8,512,1024]{3,2,1,0:T(8,128)}, bf16[8,512,1024]{2,1,0:T(8,128)(2,1)S(1)}) fusion(f32[8,512,1024]{2,1,0:T(8,128)} %get-tuple-element.66, f32[8,512]{1,0:T(8,128)S(1)} %get-tuple-element.65, f32[8,512,1024]{2,1,0:T(8,128)} %get-tuple-element.60, f32[8,512]{1,0:T(8,128)S(1)} %log_add_fusion), kind=kLoop, calls=%fused_computation.77 | loop fusion | flops 16777216 | bytes 58753024
  790.4 4.2 convolution_convert_fusion.7
  794.6 6.2 fusion.69
  803.7 4.2 convolution_convert_fusion.8
  809.2 24.5 %reduce-scatter.20.cloned.1.call-done = bf16[1280,256]{1,0:T(8,128)(2,1)} async-done(((bf16[1280,2048]{1,0:T(8,128)(2,1)}), bf16[1280,256]{1,0:T(8,128)(2,1)}) %reduce-scatter.20.cloned.1.call-update) | async-done | bytes 655376 | tf_op jit(solution)/shard_map/reduce_scatter | solution.py:256
  834.0 44.1 %reduce-scatter.12.cloned.1.call-done = bf16[256,512]{1,0:T(8,128)(2,1)} async-done(((bf16[2048,512]{1,0:T(8,128)(2,1)}), bf16[256,512]{1,0:T(8,128)(2,1)}) %reduce-scatter.12.cloned.1.call-update) | async-done | bytes 262160 | tf_op jit(solution)/shard_map/reduce_scatter | solution.py:244
  878.2 44.8 %reduce-scatter.14.cloned.1.call-done = bf16[512,256]{1,0:T(8,128)(2,1)} async-done(((bf16[512,2048]{1,0:T(8,128)(2,1)}), bf16[512,256]{1,0:T(8,128)(2,1)}) %reduce-scatter.14.cloned.1.call-update) | async-done | bytes 262160 | tf_op jit(solution)/shard_map/reduce_scatter | solution.py:247
  923.1 45.0 %reduce-scatter.10.cloned.1.call-done = bf16[256,512]{1,0:T(8,128)(2,1)} async-done(((bf16[2048,512]{1,0:T(8,128)(2,1)}), bf16[256,512]{1,0:T(8,128)(2,1)}) %reduce-scatter.10.cloned.1.call-update) | async-done | bytes 262160 | tf_op jit(solution)/shard_map/reduce_scatter | solution.py:241
  968.2 45.4 %reduce-scatter.8.cloned.1.call-done = bf16[256,512]{1,0:T(8,128)(2,1)} async-done(((bf16[2048,512]{1,0:T(8,128)(2,1)}), bf16[256,512]{1,0:T(8,128)(2,1)}) %reduce-scatter.8.cloned.1.call-update) | async-done | bytes 262160 | tf_op jit(solution)/shard_map/reduce_scatter | solution.py:238
  1013.7 10.1 convolution_convert_fusion.3
  1028.6 6.1 add_convert_fusion
  1034.8 6.5 convert_element_type.353
  1042.8 13.7 all-gather.19.cloned.1.call-done
  1056.5 7.4 convert_element_type.421
  1063.8 35.7 %all-gather.21.cloned.1.call-done = bf16[2048,1280]{1,0:T(8,128)(2,1)} async-done(((bf16[256,1280]{1,0:T(8,128)(2,1)}), bf16[2048,1280]{1,0:T(8,128)(2,1)}) %all-gather.21.cloned.1.call-update) | async-done | bytes 5242896 | tf_op jit(solution)/shard_map/all_gather | solution.py:279
  1099.5 7.4 convert_element_type.423
  1106.9 36.4 %all-gather.23.cloned.1.call-done = bf16[1280,2048]{1,0:T(8,128)(2,1)} async-done(((bf16[1280,256]{1,0:T(8,128)(2,1)}), bf16[1280,2048]{1,0:T(8,128)(2,1)}) %all-gather.23.cloned.1.call-update) | async-done | bytes 5242896 | tf_op jit(solution)/shard_map/all_gather | solution.py:282
  1143.3 8.2 convert_element_type.425
  1151.5 5.3 convert_element_type.391
  1156.8 18.6 %copy.33 = f32[1,8,512,1024]{3,1,2,0:T(8,128)} copy(f32[1,8,512,1024]{3,2,1,0:T(8,128)} %get-tuple-element.40) | data formatting | bytes 33554432
  1175.4 20.9 %copy.34 = f32[1,8,512,1024]{3,1,2,0:T(8,128)} copy(f32[1,8,512,1024]{3,2,1,0:T(8,128)S(1)} %bitcast.185) | data formatting | bytes 33554432
  1196.4 34.5 %fusion = f32[32,8]{1,0:T(8,128)S(1)} fusion(f32[8,524288]{1,0:T(8,128)} %bitcast.192, s32[524288]{0:T(1024)S(1)} %copy-done.18), kind=kOutput, calls=%fused_computation.1 | convolution fusion | flops 1627389952 | bytes 18875392 | tf_op jit(solution)/shard_map/dot_general | solution.py:214
  1230.9 34.6 %fusion.74 = bf16[32,8]{1,0:T(8,128)(2,1)S(1)} fusion(f32[32,8]{1,0:T(8,128)S(1)} %fusion, f32[8,524288]{1,0:T(8,128)} %bitcast.191, s32[524288]{0:T(1024)S(1)} %copy-done.20), kind=kOutput, calls=%fused_computation.129 | convolution fusion | flops 1627390464 | bytes 18875904 | tf_op jit(solution)/shard_map/dot_general | solution.py:214
  1265.5 13.8 all-reduce
  1279.3 8.9 all-gather.1
  1288.9 4.2 convert_element_type.417
  1293.1 4.1 convert_element_type.419
  1297.2 4.2 convert_element_type.415
  1301.4 4.2 convert_element_type.413
  1305.6 250.9 %all-reduce.8.cloned.1.call-done = (bf16[1024,2048]{1,0:T(8,128)(2,1)}, bf16[1024,2048]{1,0:T(8,128)(2,1)}) async-done(((bf16[1024,2048]{1,0:T(8,128)(2,1)}, bf16[1024,2048]{1,0:T(8,128)(2,1)}), (bf16[1024,2048]{1,0:T(8,128)(2,1)}, bf16[1024,2048]{1,0:T(8,128)(2,1)})) %all-reduce.8.cloned.1.call-update) | async-done | bytes 8388624 | tf_op jit(solution)/shard_map/psum | solution.py:138
  1556.5 10.2 fusion.21
  1567.8 7.0 fusion.56
  1574.8 39.4 %all-reduce.1 = (f32[2048]{0:T(1024)}, f32[2048]{0:T(1024)}) all-reduce(f32[2048]{0:T(1024)S(1)} %get-tuple-element.57, f32[2048]{0:T(1024)S(1)} %get-tuple-element.70), channel_id=1, replica_groups=mesh['dp'=8,'tensor'=4] {'dp','tensor'}, use_global_device_ids=true, to_apply=%region_22.23 | all-reduce | flops 4096 | bytes 32768 | tf_op jit(solution)/shard_map/psum | solution.py:236
  (218 shorter events, 63.6 us)
Async XLA Ops:
  7.2 139.3 %copy-start = (bf16[512,2048]{1,0:T(8,128)(2,1)S(1)}, bf16[512,2048]{1,0:T(8,128)(2,1)}, u32[]{:S(2)}) copy-start(bf16[512,2048]{1,0:T(8,128)(2,1)} %param.19) | copy-start | bytes 6291460
  7.2 301.6 %all-reduce.6.cloned.1.call-start = ((), (), s32[]{:S(2)}) async-start(), calls=%async_computation.7 | async-start | bytes 8388608 | tf_op jit(solution)/shard_map/psum | solution.py:130
  10.5 6.7 copy-start.44
  13.1 96.3 %copy-start.21 = (bf16[1024,512]{0,1:T(8,128)(2,1)}, bf16[1024,512]{0,1:T(8,128)(2,1)S(1)}, u32[]{:S(2)}) copy-start(bf16[1024,512]{0,1:T(8,128)(2,1)S(1)} %convolution_convert_fusion.10) | copy-start | bytes 3145732
  15.7 93.7 %copy-start.14 = (bf16[1024,512]{0,1:T(8,128)(2,1)}, bf16[1024,512]{0,1:T(8,128)(2,1)S(1)}, u32[]{:S(2)}) copy-start(bf16[1024,512]{0,1:T(8,128)(2,1)S(1)} %convolution_convert_fusion.9) | copy-start | bytes 3145732
  24.2 23.3 %copy-start.17 = (s32[524288]{0:T(1024)}, s32[524288]{0:T(1024)S(1)}, u32[]{:S(2)}) copy-start(s32[524288]{0:T(1024)S(1)} %fusion.51) | copy-start | bytes 6291460
  49.1 23.7 %copy-start.19 = (s32[524288]{0:T(1024)}, s32[524288]{0:T(1024)S(1)}, u32[]{:S(2)}) copy-start(s32[524288]{0:T(1024)S(1)} %fusion.50) | copy-start | bytes 6291460
  73.4 29.4 %copy-start.28 = (bf16[1024,512]{0,1:T(8,128)(2,1)S(1)}, bf16[1024,512]{0,1:T(8,128)(2,1)}, u32[]{:S(2)}) copy-start(bf16[1024,512]{0,1:T(8,128)(2,1)} %convolution_convert_fusion.11) | copy-start | bytes 3145732
  94.9 7.9 copy-start.39
  94.9 10.6 copy-start.2
  102.8 6.6 copy-start.42
  131.0 10.6 copy-start.3
  150.9 162.9 %copy-start.41 = (f32[2048]{0:T(1024)S(1)}, f32[2048]{0:T(1024)}, u32[]{:S(2)}) copy-start(f32[2048]{0:T(1024)} %param.24) | copy-start | bytes 24580
  150.9 503.6 %all-gather.25.cloned.1.call-start = ((), (), s32[]{:S(2)}) async-start(), calls=%async_computation.22 | async-start | bytes 20971520 | tf_op jit(solution)/shard_map/all_gather | solution.py:153
  308.8 5.1 copy-start.5
  308.8 5.9 copy-start.13
  308.8 8.7 slice-start.8
  317.5 18.7 %copy-start.24 = (bf16[1024,2048]{1,0:T(8,128)(2,1)}, bf16[1024,2048]{1,0:T(8,128)(2,1)S(1)}, u32[]{:S(2)}) copy-start(bf16[1024,2048]{1,0:T(8,128)(2,1)S(1)} %multiply_convert_fusion) | copy-start | bytes 12582916
  317.5 7.3 copy-start.30
  336.2 21.1 %copy-start.56 = (bf16[1024,1280]{1,0:T(8,128)(2,1)}, bf16[1024,1280]{1,0:T(8,128)(2,1)S(1)}, u32[]{:S(2)}) copy-start(bf16[1024,1280]{1,0:T(8,128)(2,1)S(1)} %get-tuple-element.63) | copy-start | bytes 7864324
  349.5 7.9 copy-start.57
  368.6 439.4 %reduce-scatter.16.cloned.1.call-start = ((), (), s32[]{:S(2)}) async-start(), calls=%async_computation.16 | async-start | bytes 5898240 | tf_op jit(solution)/shard_map/reduce_scatter | solution.py:250
  378.4 430.1 %reduce-scatter.18.cloned.1.call-start = ((), (), s32[]{:S(2)}) async-start(), calls=%async_computation.18 | async-start | bytes 5898240 | tf_op jit(solution)/shard_map/reduce_scatter | solution.py:253
  389.1 444.6 %reduce-scatter.20.cloned.1.call-start = ((), (), s32[]{:S(2)}) async-start(), calls=%async_computation.20 | async-start | bytes 5898240 | tf_op jit(solution)/shard_map/reduce_scatter | solution.py:256
  389.1 9.3 copy-start.25
  398.4 10.6 copy-start.31
  416.5 461.6 %reduce-scatter.12.cloned.1.call-start = ((), (), s32[]{:S(2)}) async-start(), calls=%async_computation.12 | async-start | bytes 2359296 | tf_op jit(solution)/shard_map/reduce_scatter | solution.py:244
  667.0 7.8 copy-start.6
  674.9 19.7 %slice-start = ((s8[16777216]{0:T(1024)(128)(4,1)}), s8[4194304]{0:T(1024)(128)(4,1)S(1)}, s32[]{:S(2)}) async-start(s8[16777216]{0:T(1024)(128)(4,1)} %bitcast.180), calls=%async_computation.24 | async-start | bytes 8388608
  674.9 19.7 %slice-start.1 = ((s8[16777216]{0:T(1024)(128)(4,1)}), s8[4194304]{0:T(1024)(128)(4,1)S(1)}, s32[]{:S(2)}) async-start(s8[16777216]{0:T(1024)(128)(4,1)} %bitcast.180), calls=%async_computation.25 | async-start | bytes 8388608
  674.9 19.7 %slice-start.2 = ((s8[16777216]{0:T(1024)(128)(4,1)}), s8[4194304]{0:T(1024)(128)(4,1)S(1)}, s32[]{:S(2)}) async-start(s8[16777216]{0:T(1024)(128)(4,1)} %bitcast.180), calls=%async_computation.26 | async-start | bytes 8388608
  688.5 6.1 slice-start.3
  694.5 17.0 %copy-start.23 = (bf16[1024,512]{0,1:T(8,128)(2,1)}, bf16[1024,512]{0,1:T(8,128)(2,1)S(1)}, u32[]{:S(2)}) copy-start(bf16[1024,512]{0,1:T(8,128)(2,1)S(1)} %fusion.64) | copy-start | bytes 3145732
  698.0 9.4 copy-start.45
  698.0 9.4 copy-start.49
  722.9 200.1 %reduce-scatter.14.cloned.1.call-start = ((), (), s32[]{:S(2)}) async-start(), calls=%async_computation.14 | async-start | bytes 2359296 | tf_op jit(solution)/shard_map/reduce_scatter | solution.py:247
  723.0 22.8 %copy-start.22 = (bf16[1024,512]{0,1:T(8,128)(2,1)S(1)}, bf16[1024,512]{0,1:T(8,128)(2,1)}, u32[]{:S(2)}) copy-start(bf16[1024,512]{0,1:T(8,128)(2,1)} %copy-done.21) | copy-start | bytes 3145732
  766.3 201.7 %reduce-scatter.10.cloned.1.call-start = ((), (), s32[]{:S(2)}) async-start(), calls=%async_computation.10 | async-start | bytes 2359296 | tf_op jit(solution)/shard_map/reduce_scatter | solution.py:241
  784.4 4.6 copy-start.9
  784.4 5.9 copy-start.7
  790.4 4.3 copy-start.15
  794.6 219.0 %reduce-scatter.8.cloned.1.call-start = ((), (), s32[]{:S(2)}) async-start(), calls=%async_computation.8 | async-start | bytes 2359296 | tf_op jit(solution)/shard_map/reduce_scatter | solution.py:238
  794.6 6.2 copy-start.10
  803.7 4.2 copy-start.37
  807.9 248.6 %all-gather.19.cloned.1.call-start = ((), (), s32[]{:S(2)}) async-start(), calls=%async_computation.17 | async-start | bytes 5898240 | tf_op jit(solution)/shard_map/all_gather | solution.py:276
  808.5 291.0 %all-gather.21.cloned.1.call-start = ((), (), s32[]{:S(2)}) async-start(), calls=%async_computation.19 | async-start | bytes 5898240 | tf_op jit(solution)/shard_map/all_gather | solution.py:279
  809.2 334.1 %all-gather.23.cloned.1.call-start = ((), (), s32[]{:S(2)}) async-start(), calls=%async_computation.21 | async-start | bytes 5898240 | tf_op jit(solution)/shard_map/all_gather | solution.py:282
  833.8 455.1 %all-gather.15.cloned.1.call-start = ((), (), s32[]{:S(2)}) async-start(), calls=%async_computation.13 | async-start | bytes 2359296 | tf_op jit(solution)/shard_map/all_gather | solution.py:270
  878.1 414.9 %all-gather.17.cloned.1.call-start = ((), (), s32[]{:S(2)}) async-start(), calls=%async_computation.15 | async-start | bytes 2359296 | tf_op jit(solution)/shard_map/all_gather | solution.py:273
  923.0 374.2 %all-gather.13.cloned.1.call-start = ((), (), s32[]{:S(2)}) async-start(), calls=%async_computation.11 | async-start | bytes 2359296 | tf_op jit(solution)/shard_map/all_gather | solution.py:267
  968.1 333.3 %all-gather.11.cloned.1.call-start = ((), (), s32[]{:S(2)}) async-start(), calls=%async_computation.9 | async-start | bytes 2359296 | tf_op jit(solution)/shard_map/all_gather | solution.py:264
  1013.6 10.2 copy-start.33
  1013.6 542.8 %all-reduce.8.cloned.1.call-start = ((), (), s32[]{:S(2)}) async-start(), calls=%async_computation.23 | async-start | bytes 16777216 | tf_op jit(solution)/shard_map/psum | solution.py:138
  1013.7 10.1 copy-start.51
  1034.8 6.6 copy-start.54
  1143.3 8.2 copy-start.12
  1151.5 23.9 %slice-start.4 = ((s8[16777216]{0:T(1024)(128)(4,1)}), s8[4194304]{0:T(1024)(128)(4,1)S(1)}, s32[]{:S(2)}) async-start(s8[16777216]{0:T(1024)(128)(4,1)} %bitcast.184), calls=%async_computation.28 | async-start | bytes 8388608
  1151.5 23.9 %slice-start.5 = ((s8[16777216]{0:T(1024)(128)(4,1)}), s8[4194304]{0:T(1024)(128)(4,1)S(1)}, s32[]{:S(2)}) async-start(s8[16777216]{0:T(1024)(128)(4,1)} %bitcast.184), calls=%async_computation.29 | async-start | bytes 8388608
  1156.8 18.6 %slice-start.6 = ((s8[16777216]{0:T(1024)(128)(4,1)}), s8[4194304]{0:T(1024)(128)(4,1)S(1)}, s32[]{:S(2)}) async-start(s8[16777216]{0:T(1024)(128)(4,1)} %bitcast.184), calls=%async_computation.30 | async-start | bytes 8388608
  1156.8 18.6 %slice-start.7 = ((s8[16777216]{0:T(1024)(128)(4,1)}), s8[4194304]{0:T(1024)(128)(4,1)S(1)}, s32[]{:S(2)}) async-start(s8[16777216]{0:T(1024)(128)(4,1)} %bitcast.184), calls=%async_computation.31 | async-start | bytes 8388608
  1175.4 21.0 %copy-start.18 = (s32[524288]{0:T(1024)S(1)}, s32[524288]{0:T(1024)}, u32[]{:S(2)}) copy-start(s32[524288]{0:T(1024)} %copy-done.17) | copy-start | bytes 6291460
  1196.4 34.5 %copy-start.20 = (s32[524288]{0:T(1024)S(1)}, s32[524288]{0:T(1024)}, u32[]{:S(2)}) copy-start(s32[524288]{0:T(1024)} %copy-done.19) | copy-start | bytes 6291460
  1556.5 10.2 copy-start.16
  1567.8 46.3 %copy-start.1 = (bf16[512,2048]{1,0:T(8,128)(2,1)S(1)}, bf16[512,2048]{1,0:T(8,128)(2,1)}, u32[]{:S(2)}) copy-start(bf16[512,2048]{1,0:T(8,128)(2,1)} %param.19) | copy-start | bytes 6291460
  (21 other events, 44.3 us)
Sparse Core Ops, SparseCore 0:
  151.0 157.6 all-reduce.5
  368.7 285.7 all-gather.24
  658.9 54.7 reduce-scatter.15
  716.9 56.5 reduce-scatter.17
  777.1 56.5 reduce-scatter.19
  836.9 41.1 reduce-scatter.11
  881.7 41.2 reduce-scatter.13
  926.9 41.1 reduce-scatter.9
  972.3 41.2 reduce-scatter.7
  1015.3 41.1 all-gather.18
  1058.3 41.1 all-gather.20
  1101.2 42.0 all-gather.22
  1145.2 27.8 all-gather.14
  1174.9 28.1 all-gather.16
  1204.8 27.8 all-gather.12
  1234.5 27.8 all-gather.10
  1264.9 291.5 all-reduce.7
